TPU v7x, 256 devices: a whole 4x4x8 slice. The times are simulated.
256 devices in a mesh: energy: 64 (over x, z_hi, y), space: 4 (over z_lo, core).
Axes of the slice: x: 4, y: 4, z: 8 (z_hi: 4, z_lo: 2; z = z_hi * 2 + z_lo), core: 2. Of those that a mesh axis runs over, the one named last changes fastest.
Arguments:
- g_lesser: bfloat16 [64, 2, 4, 512, 512], P('energy', None, 'space'), may hold values from -6 to 6, as said below
- w_lesser: bfloat16 [64, 2, 4, 512, 512], P('energy', None, 'space'), may hold values from -6 to 6, as said below
- g_retarded: bfloat16 [64, 2, 4, 4, 512, 512], P('energy', None, 'space'), may hold values from -0.1875 to 0.1875
- energy_index: int32 [64], replicated, may hold values from 0 to 63, each once
Outputs:
- sigma_lesser: bfloat16 [64, 2, 4, 512, 512], P('energy', None, 'space')
- delta_green: bfloat16 [64, 2, 4, 512, 512], P('energy', None, 'space')
Inputs may be any that keep to these rules, and one draw needn't show every extreme that they name: `g_lesser`: anti-Hermitian in every diagonal block at every energy: element (j, i) of component 0 is minus element (i, j), of component 1 equal to it. `w_lesser`: anti-Hermitian in every diagonal block at every energy: element (j, i) of component 0 is minus element (i, j), of component 1 equal to it. `energy_index`: each grid point once.
All inputs are finite; a program needn't handle non-finite values.
Results may differ from a plain program's by a relative error of at most 0.013.
Values may be sent and summed in bfloat16 or wider, within the bound.
A program may use at most 128 MiB of HBM per device.

v0:
```python
import math

import jax
import jax.numpy as jnp
from jax import lax
from jax.sharding import PartitionSpec as P


def twiddles(energy_index, per_device, groups):
    grid_size = energy_index.shape[0]
    padded_len = 2 * grid_size
    row_count = 2 * grid_size
    row_ids = lax.iota(jnp.int32, row_count)
    local_energy = row_ids // (2 * groups)
    component = row_ids // groups % 2
    source = row_ids % groups
    stored = source * per_device + local_energy
    grid_point = energy_index[stored]
    frequency = lax.iota(jnp.int32, padded_len)
    forward_phase = frequency[:, None] * grid_point[None, :] % padded_len
    forward_angle = forward_phase.astype(jnp.float32) * (2.0 * math.pi / padded_len)
    cos_fwd = jnp.cos(forward_angle)
    sin_fwd = jnp.sin(forward_angle)
    real_column = (component == 0)[None, :]
    forward = jnp.concatenate(
        [jnp.where(real_column, cos_fwd, sin_fwd), jnp.where(real_column, -sin_fwd, cos_fwd)],
        axis=0,
    )
    shifted = grid_point + grid_size // 2
    backward_phase = shifted[:, None] * frequency[None, :] % padded_len
    backward_angle = backward_phase.astype(jnp.float32) * (2.0 * math.pi / padded_len)
    cos_back = jnp.cos(backward_angle)
    sin_back = jnp.sin(backward_angle)
    real_row = (component == 0)[:, None]
    factor = grid_size ** (-0.5) / padded_len
    left_half = jnp.where(real_row, -sin_back, cos_back) * factor
    right_half = jnp.where(real_row, -cos_back, -sin_back) * factor
    backward = jnp.concatenate([left_half, right_half], axis=1)
    return (forward, backward)


def transform(matrix_high, matrix_low, operand):
    return jnp.dot(matrix_high, operand, preferred_element_type=jnp.float32) + jnp.dot(
        matrix_low, operand, preferred_element_type=jnp.float32
    )


def convolve(green_rows, screen_rows, forward, backward):
    padded_len = forward.shape[0] // 2
    forward_high = forward.astype(jnp.bfloat16)
    forward_low = (forward - forward_high.astype(jnp.float32)).astype(jnp.bfloat16)
    green_hat = transform(forward_high, forward_low, green_rows)
    screen_hat = transform(forward_high, forward_low, screen_rows)
    green_real = green_hat[:padded_len]
    green_imag = green_hat[padded_len:]
    screen_real = screen_hat[:padded_len]
    screen_imag = screen_hat[padded_len:]
    prod_real = green_real * screen_real - green_imag * screen_imag
    prod_imag = green_real * screen_imag + green_imag * screen_real
    merged = jnp.concatenate([prod_real, prod_imag], axis=0)
    return jnp.dot(backward, merged, precision=lax.Precision.HIGH).astype(jnp.bfloat16)


def shards(g_lesser, w_lesser, g_retarded, energy_index):
    energies_here = g_lesser.shape[0]
    width = g_lesser.shape[3]
    groups = lax.axis_size("energy")
    forward, backward = twiddles(energy_index, energies_here, groups)
    own_row = g_retarded[:, :, 0]
    columns = width * width // groups
    green = g_lesser.reshape(energies_here, 2, groups, columns)
    screen = w_lesser.reshape(energies_here, 2, groups, columns)
    green_el, screen_el = (
        lax.all_to_all(green, "energy", split_axis=2, concat_axis=2, tiled=True),
        lax.all_to_all(screen, "energy", split_axis=2, concat_axis=2, tiled=True),
    )
    sigma_el = convolve(
        green_el.reshape(-1, columns), screen_el.reshape(-1, columns), forward, backward
    )
    sigma_el = sigma_el.reshape(energies_here, 2, groups, columns)
    sigma_back = lax.all_to_all(sigma_el, "energy", split_axis=2, concat_axis=2, tiled=True)
    sigma_lesser = sigma_back.reshape(energies_here, 2, 1, width, width)
    first_prod = jnp.einsum(
        "ecnij,ednjl->encdil",
        own_row,
        lax.all_gather(sigma_lesser, "space", axis=2, tiled=True),
        preferred_element_type=jnp.float32,
    )
    left_product = jnp.stack(
        [
            first_prod[:, :, 0, 0] - first_prod[:, :, 1, 1],
            first_prod[:, :, 0, 1] + first_prod[:, :, 1, 0],
        ],
        axis=1,
    ).astype(jnp.bfloat16)
    second_prod = jnp.einsum(
        "ecnil,ednml->ecdim", left_product, own_row, preferred_element_type=jnp.float32
    )
    out_real = second_prod[:, 0, 0] + second_prod[:, 1, 1]
    out_imag = second_prod[:, 1, 0] - second_prod[:, 0, 1]
    delta = jnp.stack([out_real, out_imag], axis=1)
    delta_green = delta.astype(jnp.bfloat16).reshape(energies_here, 2, 1, width, width)
    return (sigma_lesser, delta_green)


def solution(mesh):
    return jax.shard_map(
        shards,
        mesh=mesh,
        in_specs=(
            P("energy", None, "space", None, None),
            P("energy", None, "space", None, None),
            P("energy", None, "space", None, None, None),
            P(),
        ),
        out_specs=(P("energy", None, "space", None, None), P("energy", None, "space", None, None)),
        check_vma=False,
    )
```

profile of v0, /device:TPU:1, one launch (start us, length us, event | category | flops | bytes accessed | tf_op | source)
XLA Modules:
  0.0 215.1 jit_solution(1046797866290290498)
XLA Ops:
  7.2 0.0 copy-start
  7.2 0.0 copy-start.4
  7.2 1.6 reshape.274
  8.8 2.1 copy.28
  10.9 15.1 %all-to-all-start.1 = ((bf16[1,2,64,4096]{3,1,0,2:T(2,128)(2,1)}), bf16[1,2,64,4096]{3,1,0,2:T(2,128)(2,1)S(1)}, u32[]{:S(2)}, u32[]{:S(2)}) async-start(bf16[1,2,64,4096]{3,1,0,2:T(2,128)(2,1)} %copy.28), calls=%async_computation.1 | async-start | bytes 2097152 | tf_op jit(solution)/shard_map/all_to_all | solution.py:75
  26.0 0.0 copy-done.4
  26.0 0.5 reshape.272
  26.6 2.1 copy.26
  28.6 25.1 %all-to-all-done.1 = bf16[1,2,64,4096]{3,1,0,2:T(2,128)(2,1)S(1)} async-done(((bf16[1,2,64,4096]{3,1,0,2:T(2,128)(2,1)}), bf16[1,2,64,4096]{3,1,0,2:T(2,128)(2,1)S(1)}, u32[]{:S(2)}, u32[]{:S(2)}) %all-to-all-start.1) | async-done | bytes 1048608 | tf_op jit(solution)/shard_map/all_to_all | solution.py:75
  53.7 8.3 %all-to-all-start = ((bf16[1,2,64,4096]{3,1,0,2:T(2,128)(2,1)}), bf16[1,2,64,4096]{3,1,0,2:T(2,128)(2,1)S(1)}, u32[]{:S(2)}, u32[]{:S(2)}) async-start(bf16[1,2,64,4096]{3,1,0,2:T(2,128)(2,1)} %copy.26), calls=%async_computation | async-start | bytes 2097152 | tf_op jit(solution)/shard_map/all_to_all | solution.py:74
  62.0 0.2 all-gather.2.cloned.1.call-start
  62.3 0.0 copy-done
  62.3 1.2 gather_fusion
  63.6 0.6 select_multiply_fusion.1
  64.2 0.6 copy.29
  64.8 0.7 fusion.36
  65.5 2.6 %convolution_add_fusion = f32[256,4096]{1,0:T(8,128)} fusion(f32[256,4096]{1,0:T(8,128)S(1)} %fusion.36, bf16[128,4096]{1,0:T(8,128)(2,1)S(1)} %bitcast.74, f32[128,128]{1,0:T(8,128)S(1)} %get-tuple-element.18, f32[128,128]{1,0:T(8,128)S(1)} %get-tuple-element.19), kind=kOutput, calls=%fused_computation.2 | convolution fusion | flops 269647872 | bytes 9568256 | tf_op jit(solution)/shard_map/dot_general | solution.py:43
  68.1 22.7 %all-to-all-done = bf16[1,2,64,4096]{3,1,0,2:T(2,128)(2,1)S(1)} async-done(((bf16[1,2,64,4096]{3,1,0,2:T(2,128)(2,1)}), bf16[1,2,64,4096]{3,1,0,2:T(2,128)(2,1)S(1)}, u32[]{:S(2)}, u32[]{:S(2)}) %all-to-all-start) | async-done | bytes 1048608 | tf_op jit(solution)/shard_map/all_to_all | solution.py:74
  90.8 0.6 copy.27
  91.3 0.7 fusion.38
  92.0 0.0 copy-start.2
  92.0 0.7 convolution_add_fusion.1
  92.8 1.5 copy-done.2
  94.2 0.9 multiply_subtract_fusion
  95.2 1.5 convolution_convert_fusion
  96.7 1.1 copy.30
  97.8 32.1 %all_to_all.15 = bf16[1,2,64,4096]{3,1,0,2:T(2,128)(2,1)S(1)} all-to-all(bf16[1,2,64,4096]{3,1,0,2:T(2,128)(2,1)S(1)} %copy.30), channel_id=1, replica_groups=mesh['energy'=64,'space'=4] {'energy'}, dimensions={2} | all-to-all | bytes 2097152 | tf_op jit(solution)/shard_map/all_to_all | solution.py:81
  130.0 0.6 copy.31
  130.6 1.3 reshape.277
  131.9 0.0 all-gather.2.cloned.1.call-update
  131.9 47.4 %all-gather.2.cloned.1.call-done = bf16[1,2,4,512,512]{4,3,1,0,2:T(8,128)(2,1)} async-done(((bf16[1,2,1,512,512]{4,3,1,0,2:T(8,128)(2,1)}), bf16[1,2,4,512,512]{4,3,1,0,2:T(8,128)(2,1)}) %all-gather.2.cloned.1.call-update) | async-done | bytes 4194320 | tf_op jit(solution)/shard_map/all_gather | solution.py:86
  179.3 14.1 %convolution_bitcast_fusion = f32[1,4,2,2,512,512]{4,5,2,3,1,0:T(8,128)} fusion(bf16[1,2,4,512,512]{4,3,1,0,2:T(8,128)(2,1)} %all-gather.2.cloned.1.call-done, bf16[1,2,1,4,512,512]{5,4,3,2,1,0:T(8,128)(2,1)} %param.6), kind=kOutput, calls=%fused_computation.1 | convolution fusion | flops 4294967296 | bytes 25165824 | tf_op jit(solution)/shard_map/ecnij,ednjl->encdil/dot_general | solution.py:83
  193.4 4.2 %fusion.13 = bf16[1,4,512,512]{2,3,1,0:T(8,128)(2,1)S(1)} fusion(f32[1,4,2,2,512,512]{4,5,2,3,1,0:T(8,128)} %convolution_bitcast_fusion), kind=kLoop, calls=%fused_computation.22 | loop fusion | flops 2097152 | bytes 10485760 | tf_op jit(solution)/shard_map/add | solution.py:92
  197.6 0.0 copy-start.3
  197.6 4.4 %fusion.12 = bf16[1,4,512,512]{2,3,1,0:T(8,128)(2,1)S(1)} fusion(f32[1,4,2,2,512,512]{4,5,2,3,1,0:T(8,128)} %convolution_bitcast_fusion), kind=kLoop, calls=%fused_computation.21 | loop fusion | flops 2097152 | bytes 10485760 | tf_op jit(solution)/shard_map/sub | solution.py:91
  202.1 0.2 copy-done.3
  202.3 0.0 copy-start.1
  202.3 4.5 %fusion.11 = f32[1,2,2,512,512]{4,3,2,1,0:T(8,128)S(1)} fusion(bf16[1,4,512,512]{2,3,1,0:T(8,128)(2,1)S(1)} %fusion.13, bf16[1,4,512,512]{2,3,1,0:T(8,128)(2,1)S(1)} %fusion.12, bf16[1,2,1,4,512,512]{5,4,3,2,1,0:T(8,128)(2,1)S(1)} %copy-done.3), kind=kOutput, calls=%fused_computation.20 | convolution fusion | flops 4303355904 | bytes 12582912 | tf_op jit(solution)/shard_map/ecnil,ednml->ecdim/dot_general | solution.py:96
  206.8 0.4 fusion.15
  207.2 1.1 pad_maximum_fusion
  208.2 0.0 copy-done.1
  (4 shorter events, 0.0 us)
Async XLA Ops:
  7.2 55.1 %copy-start = (s32[64]{0:T(128)S(1)}, s32[64]{0:T(128)}, u32[]{:S(2)}) copy-start(s32[64]{0:T(128)} %param.7) | copy-start | bytes 772
  7.2 18.8 %copy-start.4 = (bf16[1,2,1,512,512]{4,3,2,1,0:T(8,128)(2,1)S(1)}, bf16[1,2,1,512,512]{4,3,2,1,0:T(8,128)(2,1)}, u32[]{:S(2)}) copy-start(bf16[1,2,1,512,512]{4,3,2,1,0:T(8,128)(2,1)} %param.4) | copy-start | bytes 3145732
  10.9 42.8 %all-to-all-start.1 = ((bf16[1,2,64,4096]{3,1,0,2:T(2,128)(2,1)}), bf16[1,2,64,4096]{3,1,0,2:T(2,128)(2,1)S(1)}, u32[]{:S(2)}, u32[]{:S(2)}) async-start(bf16[1,2,64,4096]{3,1,0,2:T(2,128)(2,1)} %copy.28), calls=%async_computation.1 | async-start | bytes 2097152 | tf_op jit(solution)/shard_map/all_to_all | solution.py:75
  53.7 37.0 %all-to-all-start = ((bf16[1,2,64,4096]{3,1,0,2:T(2,128)(2,1)}), bf16[1,2,64,4096]{3,1,0,2:T(2,128)(2,1)S(1)}, u32[]{:S(2)}, u32[]{:S(2)}) async-start(bf16[1,2,64,4096]{3,1,0,2:T(2,128)(2,1)} %copy.26), calls=%async_computation | async-start | bytes 2097152 | tf_op jit(solution)/shard_map/all_to_all | solution.py:74
  62.0 117.3 %all-gather.2.cloned.1.call-start = ((), (), s32[]{:S(2)}) async-start(), calls=%async_computation.3 | async-start | bytes 5242880 | tf_op jit(solution)/shard_map/all_gather | solution.py:86
  92.0 2.2 %copy-start.2 = (f32[256,4096]{1,0:T(8,128)S(1)}, f32[256,4096]{1,0:T(8,128)}, u32[]{:S(2)}) copy-start(f32[256,4096]{1,0:T(8,128)} %convolution_add_fusion) | copy-start | bytes 12582916
  197.6 4.6 %copy-start.3 = (bf16[1,2,1,4,512,512]{5,4,3,2,1,0:T(8,128)(2,1)S(1)}, bf16[1,2,1,4,512,512]{5,4,3,2,1,0:T(8,128)(2,1)}, u32[]{:S(2)}) copy-start(bf16[1,2,1,4,512,512]{5,4,3,2,1,0:T(8,128)(2,1)} %param.6) | copy-start | bytes 12582916
  202.3 6.0 %copy-start.1 = (s32[64]{0:T(128)S(1)}, s32[64]{0:T(128)}, u32[]{:S(2)}) copy-start(s32[64]{0:T(128)} %param.7) | copy-start | bytes 772
Sparse Core Ops, SparseCore 0:
  132.0 47.2 all-gather.1
where the time goes:
time: 215 us
  waiting for transfers between devices  95.2 us (44%)
  blocking collectives  32.1 us (15%)
  matrix products  24.9 us (12%)
  starting transfers between devices  23.7 us (11%)
  between operations  14.2 us (7%)
  local copies, waits for them, and re-layouts  13.4 us (6%)
  other arithmetic  11.6 us (5%)
    all_gather x1, waiting for transfers between devices, shards(): lax.all_gather(sigma_lesser, 'space', axis=2, tiled=True)  47.4 us
    all_to_all x1, blocking collectives, shards(): lax.all_to_all(sigma_el, 'energy', split_axis=2, concat_axis=2, tiled=True)  32.1 us
    all_to_all x1, waiting for transfers between devices, shards(): lax.all_to_all(screen, 'energy', split_axis=2, concat_axis=2, tiled=True)  25.1 us
    all_to_all x1, waiting for transfers between devices, shards(): lax.all_to_all(green, 'energy', split_axis=2, concat_axis=2, tiled=True)  22.7 us
    all_to_all x1, starting transfers between devices, shards(): lax.all_to_all(screen, 'energy', split_axis=2, concat_axis=2, tiled=True)  15.1 us
    dot_general x1, matrix products, shards(): jnp.einsum('ecnij,ednjl->encdil', own_row, lax.all_gather(sigma_lesser, '...  14.1 us
    all_to_all x1, starting transfers between devices, shards(): lax.all_to_all(green, 'energy', split_axis=2, concat_axis=2, tiled=True)  8.33 us
    dot_general x1, matrix products, shards(): jnp.einsum('ecnil,ednml->ecdim', left_product, own_row, preferred_element...  4.54 us
  transfers between devices with their start and end apart: 3, of which 3 were waited for; matrix products, arithmetic and copies ran while one was open for 4% of the time, Pallas kernels for 0%

commit v1 on v0

v1 whole, which is shorter than its diff:
```python
import functools
import math

import jax
import jax.numpy as jnp
import numpy as np
from jax import lax
from jax.experimental import pallas as pl
from jax.experimental.pallas import tpu as pltpu
from jax.sharding import PartitionSpec as P

MESH = pl.DeviceIdType.MESH
NE = 64
B = 512
T = 128
LEN = 96
CHUNKS = 2
TILES = (((0, 0), (0, 1), (0, 2), (1, 2)), ((2, 2), (0, 3), (1, 3), (2, 3)))
BF = jnp.bfloat16
F32 = jnp.float32


def tables():
    f = np.arange(LEN)[:, None]
    p = np.arange(NE)[None, :]
    ang = 2 * math.pi * ((f * p) % LEN) / LEN
    c, s = np.cos(ang), np.sin(ang)
    forward = np.block([[c, s], [-s, c]])
    ang = 2 * math.pi * ((f * (p + NE // 2)) % LEN) / LEN
    c, s = np.cos(ang).T, np.sin(ang).T
    backward = np.block([[-s, -c], [c, -s]]) * (NE**-0.5 / LEN)

    def halves(m):
        m = m.astype(np.float32)
        hi = m.astype(jnp.bfloat16)
        lo = (m - hi.astype(np.float32)).astype(jnp.bfloat16)
        return np.stack([hi, lo])

    twice = np.concatenate([np.eye(NE), np.eye(NE)], axis=1).astype(jnp.bfloat16)
    return halves(forward), halves(backward), twice


def mm(a, b):
    return jnp.dot(a, b, preferred_element_type=F32)


def iotas(n=T):
    return lax.broadcasted_iota(jnp.int32, (n, n), 0), lax.broadcasted_iota(jnp.int32, (n, n), 1)


def body(g_hbm, w_hbm, r_hbm, idx_ref, ft_ref, bt_ref, tw_ref, sig_ref, del_ref,
         g_v, w_v, r_v, rt_v, send, recv, ssend, u_v, scr, xb, ph, pl_, fm, bm, um0, um1, xr, xi,
         lsem, gws, gwr, sgs, sgr, gas, gar):
    me = lax.axis_index("energy")
    sp = lax.axis_index("space")
    sp_core = sp // 2 * 2 + (sp + 1) % 2
    sp_z = (sp + 2) % 4
    sp_zc = (sp_core + 2) % 4

    cg = pltpu.make_async_copy(g_hbm, g_v, lsem.at[0])
    cw = pltpu.make_async_copy(w_hbm, w_v, lsem.at[1])
    cr = pltpu.make_async_copy(r_hbm, r_v, lsem.at[2])
    cg.start()
    cw.start()
    cr.start()

    barrier = pltpu.get_barrier_semaphore()

    @pl.loop(1, NE)
    def _(i):
        pl.semaphore_signal(barrier, inc=1, device_id=((me + i) % NE, sp), device_id_type=MESH)

    pl.semaphore_signal(barrier, inc=1, device_id=(me, sp_core), device_id_type=MESH)
    pl.semaphore_signal(barrier, inc=1, device_id=(me, sp_z), device_id_type=MESH)

    row, col = iotas()
    cg.wait()
    cw.wait()
    for h in range(CHUNKS):
        for t, (i, j) in enumerate(TILES[h]):
            dst = pl.ds(16 * t, 16)
            for a, src in enumerate((g_v, w_v)):
                if i == j:
                    d0r = src[0, T * i:T * i + T, T * i:T * i + T].astype(F32)
                    d0i = src[1, T * i:T * i + T, T * i:T * i + T].astype(F32)
                    k = i + 1
                    d1r = src[0, T * k:T * k + T, T * k:T * k + T].astype(F32)
                    d1i = src[1, T * k:T * k + T, T * k:T * k + T].astype(F32)
                    pr = jnp.where(row < col, d0r, jnp.where(row > col, d1r, d1i))
                    pi = jnp.where(row <= col, d0i, d1i)
                    send[h, dst, a, 0] = pr.reshape(16, 8, T).astype(BF)
                    send[h, dst, a, 1] = pi.reshape(16, 8, T).astype(BF)
                else:
                    for c in range(2):
                        blk = src[c, T * i:T * i + T, T * j:T * j + T].astype(F32)
                        send[h, dst, a, c] = blk.reshape(16, 8, T).astype(BF)

    pl.semaphore_wait(barrier, NE + 1)

    for h in range(CHUNKS):
        @pl.loop(1, NE)
        def _(i):
            d = (me + i) % NE
            pltpu.make_async_remote_copy(
                src_ref=send.at[h, d], dst_ref=recv.at[h, me], send_sem=gws.at[h], recv_sem=gwr.at[h],
                device_id=(d, sp), device_id_type=MESH).start()

        pltpu.make_async_copy(send.at[h, me], recv.at[h, me], gwr.at[h]).start()

    idx = jnp.broadcast_to(idx_ref[...].astype(F32), (8, NE)).astype(BF)
    both = mm(idx, tw_ref[...])[0:1, :]
    point = (row % NE).astype(F32)
    pick = jnp.where((point == both) & (row // NE == col // NE), 1.0, 0.0).astype(BF)
    for a in range(2):
        fm[a] = mm(ft_ref[a], pick).astype(BF)
        bm[a] = lax.dot_general(pick, bt_ref[a], (((0,), (0,)), ((), ())), preferred_element_type=F32).astype(BF)

    zero = jnp.zeros((T, T), BF)
    for c in range(2):
        um0[c, T:, :T] = zero
        um1[c, 3 * T:, :T] = zero
    xr[...] = jnp.zeros_like(xr)
    xi[...] = jnp.zeros_like(xi)
    cr.wait()

    @pl.loop(0, 8)
    def _(q):
        for i in range(4):
            for j in range(4):
                blk = r_v[q, T * i:T * i + T, T * j:T * j + T].astype(F32)
                rt_v[q, T * j:T * j + T, T * i:T * i + T] = blk.T.astype(BF)

    lane8 = lax.broadcasted_iota(jnp.int32, (T, T), 1)
    base = me % 16 * 8
    for h in range(CHUNKS):
        pltpu.make_async_copy(recv.at[h], recv.at[h], gwr.at[h]).wait()
        for a in range(2):
            for c in range(2):
                blk = recv[h, :, a, c].astype(F32)
                scr[a, c * 512:c * 512 + 512, :] = blk.reshape(512, T)
        for a in range(2):
            diag = jnp.zeros((T, T), F32)
            for i in range(8):
                x_i = scr[a, pl.ds(i, T, stride=8), :]
                diag = jnp.where(lane8 == base + i, x_i, diag)
                xb[a, :, T * i:T * i + T] = x_i.astype(BF)
            xb[a, :, 8 * T:9 * T] = jnp.where(row < NE, diag, 0.0).astype(BF)
            xb[a, :, 9 * T:] = jnp.where(row < NE, 0.0, diag).astype(BF)
        for n in range(5):
            cols = slice(256 * n, 256 * n + 256)
            gx = xb[0, :, cols]
            wx = xb[1, :, cols]
            gh = mm(fm[0], gx) + mm(fm[1], gx)
            wh = mm(fm[0], wx) + mm(fm[1], wx)
            pr = gh[:LEN] * wh[:LEN] - gh[LEN:] * wh[LEN:]
            pi = gh[:LEN] * wh[LEN:] + gh[LEN:] * wh[:LEN]
            prod = jnp.concatenate([pr, pi], axis=0)
            hi = prod.astype(BF)
            ph[:, cols] = hi
            pl_[:, cols] = (prod - hi.astype(F32)).astype(BF)
        tail = slice(8 * T, 10 * T)
        y = mm(bm[0], ph[:, tail]) + mm(bm[1], ph[:, tail]) + mm(bm[0], pl_[:, tail])
        fix = jnp.concatenate([-y[NE:, :T], y[NE:, T:]], axis=0)
        for n in range(4):
            cols = slice(256 * n, 256 * n + 256)
            y = mm(bm[0], ph[:, cols]) + mm(bm[1], ph[:, cols]) + mm(bm[0], pl_[:, cols])
            for m in range(2):
                i = 2 * n + m
                hit = (lane8 == base + i) & (me < 16)
                scr[0, pl.ds(i, T, stride=8), :] = jnp.where(hit, fix, y[:, T * m:T * m + T])
        for c in range(2):
            ssend[h, :, c] = scr[0, c * 512:c * 512 + 512, :].reshape(NE, 8, T).astype(BF)

        @pl.loop(1, NE)
        def _(i):
            d = (me + i) % NE
            pltpu.make_async_remote_copy(
                src_ref=ssend.at[h, d], dst_ref=u_v.at[sp, h, :, me], send_sem=sgs.at[h], recv_sem=sgr.at[h],
                device_id=(d, sp), device_id_type=MESH).start()

        pltpu.make_async_copy(ssend.at[h, me], u_v.at[sp, h, :, me], sgr.at[h]).start()

    def hop(k, h, lane, to):
        return pltpu.make_async_remote_copy(
            src_ref=u_v.at[k, h], dst_ref=u_v.at[k, h], send_sem=gas.at[h, lane], recv_sem=gar.at[h, lane],
            device_id=(me, to), device_id_type=MESH)

    def tile(k, h, c, t):
        return u_v[k, h, c, 16 * t:16 * t + 16].astype(F32).reshape(T, T)

    def accumulate(k, h):
        um = (um0, um1)[h]
        off = 2 * T * h
        pr = tile(k, h, 0, 0)
        pi = tile(k, h, 1, 0)
        um[0, off:off + T, 0:T] = jnp.where(row < col, pr, 0.0).astype(BF)
        um[1, off:off + T, 0:T] = jnp.where(row < col, pi, jnp.where(row == col, 0.5 * pi, 0.0)).astype(BF)
        um[0, off + T:off + 2 * T, T:] = jnp.where(row > col, pr, 0.0).astype(BF)
        um[1, off + T:off + 2 * T, T:] = jnp.where(row > col, pi, jnp.where(row == col, 0.5 * pr, 0.0)).astype(BF)
        for c in range(2):
            if h == 0:
                um[c, 0:T, T:] = tile(k, 0, c, 1).astype(BF)
            else:
                um[c, 0:T, 0:T] = tile(k, 0, c, 2).astype(BF)
                um[c, T:2 * T, 0:T] = tile(k, 0, c, 3).astype(BF)
                um[c, 0:T, T:] = tile(k, 1, c, 1).astype(BF)
                um[c, T:2 * T, T:] = tile(k, 1, c, 2).astype(BF)
                um[c, 2 * T:3 * T, T:] = tile(k, 1, c, 3).astype(BF)
        depth = 2 * T * (h + 1)

        @pl.loop(0, 2)
        def _(m):
            rows = pl.ds(pl.multiple_of(256 * m, 256), 256)
            rr = r_v[k, rows, 0:depth]
            ri = r_v[4 + k, rows, 0:depth]
            ur = um[0]
            ui = um[1]
            lr = (mm(rr, ur) - mm(ri, ui)).astype(BF)
            li = (mm(rr, ui) + mm(ri, ur)).astype(BF)
            tr = rt_v[k, off:off + 256, :]
            ti = rt_v[4 + k, off:off + 256, :]
            xr[rows, :] += mm(lr, tr) + mm(li, ti)
            xi[rows, :] += mm(li, tr) - mm(lr, ti)

    for h in range(CHUNKS):
        pltpu.make_async_copy(u_v.at[sp, h], u_v.at[sp, h], sgr.at[h]).wait()
        to_core = hop(sp, h, 0, sp_core)
        to_z = hop(sp, h, 1, sp_z)
        to_z.start()
        to_core.start()
        accumulate(sp, h)
        to_core.wait_recv()
        accumulate(sp_core, h)
        to_z.wait_recv()
        onward = hop(sp_z, h, 2, sp_core)
        onward.start()
        accumulate(sp_z, h)
        onward.wait_recv()
        accumulate(sp_zc, h)
        to_core.wait_send()
        to_z.wait_send()
        onward.wait_send()

    for h in range(CHUNKS):
        for t, (i, j) in enumerate(TILES[h]):
            pr = tile(sp, h, 0, t)
            pi = tile(sp, h, 1, t)
            prt = pr.T
            pit = pi.T
            a = slice(T * i, T * i + T)
            if i == j:
                b = slice(T * i + T, T * i + 2 * T)
                sig_ref[0, a, a] = jnp.where(row < col, pr, jnp.where(row > col, -prt, 0.0)).astype(BF)
                sig_ref[1, a, a] = jnp.where(row <= col, pi, pit).astype(BF)
                sig_ref[0, b, b] = jnp.where(row > col, pr, jnp.where(row < col, -prt, 0.0)).astype(BF)
                sig_ref[1, b, b] = jnp.where(row > col, pi, jnp.where(row < col, pit, pr)).astype(BF)
            else:
                b = slice(T * j, T * j + T)
                sig_ref[0, a, b] = pr.astype(BF)
                sig_ref[1, a, b] = pi.astype(BF)
                sig_ref[0, b, a] = (-prt).astype(BF)
                sig_ref[1, b, a] = pit.astype(BF)
    for i in range(4):
        for j in range(i, 4):
            a = slice(T * i, T * i + T)
            b = slice(T * j, T * j + T)
            dr = xr[a, b] - xr[b, a].T
            di = xi[a, b] + xi[b, a].T
            del_ref[0, a, b] = dr.astype(BF)
            del_ref[1, a, b] = di.astype(BF)
            if i != j:
                del_ref[0, b, a] = (-dr.T).astype(BF)
                del_ref[1, b, a] = di.T.astype(BF)

    for h in range(CHUNKS):
        pltpu.make_async_copy(send.at[h, 0:NE - 1], send.at[h, 0:NE - 1], gws.at[h]).wait()
        pltpu.make_async_copy(ssend.at[h, 0:NE - 1], ssend.at[h, 0:NE - 1], sgs.at[h]).wait()


def shards(g, w, r, idx):
    ft, bt, tw = tables()
    vmem = pl.BlockSpec(memory_space=pltpu.VMEM)
    hbm = pl.BlockSpec(memory_space=pl.ANY)
    out = jax.ShapeDtypeStruct((2, B, B), BF)
    dma = pltpu.SemaphoreType.DMA
    sig, delta = pl.pallas_call(
        body,
        name="gw",
        out_shape=(out, out),
        in_specs=[hbm, hbm, hbm, vmem, vmem, vmem, vmem],
        out_specs=(vmem, vmem),
        scratch_shapes=[
            pltpu.VMEM((2, B, B), BF),
            pltpu.VMEM((2, B, B), BF),
            pltpu.VMEM((8, B, B), BF),
            pltpu.VMEM((8, B, B), BF),
            pltpu.VMEM((CHUNKS, NE, 2, 2, 8, T), BF),
            pltpu.VMEM((CHUNKS, NE, 2, 2, 8, T), BF),
            pltpu.VMEM((CHUNKS, NE, 2, 8, T), BF),
            pltpu.VMEM((4, CHUNKS, 2, NE, 8, T), BF),
            pltpu.VMEM((2, 1024, T), F32),
            pltpu.VMEM((2, T, 10 * T), BF),
            pltpu.VMEM((2 * LEN, 10 * T), BF),
            pltpu.VMEM((2 * LEN, 10 * T), BF),
            pltpu.VMEM((2, 2 * LEN, T), BF),
            pltpu.VMEM((2, T, 2 * LEN), BF),
            pltpu.VMEM((2, 2 * T, 2 * T), BF),
            pltpu.VMEM((2, 4 * T, 2 * T), BF),
            pltpu.VMEM((B, B), F32),
            pltpu.VMEM((B, B), F32),
            dma((3,)),
            dma((CHUNKS,)),
            dma((CHUNKS,)),
            dma((CHUNKS,)),
            dma((CHUNKS,)),
            dma((CHUNKS, 3)),
            dma((CHUNKS, 3)),
        ],
        compiler_params=pltpu.CompilerParams(collective_id=0, has_side_effects=True,
                                             vmem_limit_bytes=48 * 1024 * 1024),
    )(g.reshape(2, B, B), w.reshape(2, B, B), r.reshape(8, B, B), idx.reshape(1, NE),
      jnp.asarray(ft), jnp.asarray(bt), jnp.asarray(tw))
    return sig.reshape(1, 2, 1, B, B), delta.reshape(1, 2, 1, B, B)


def solution(mesh):
    block = P("energy", None, "space", None, None)
    return jax.shard_map(
        shards,
        mesh=mesh,
        in_specs=(block, block, P("energy", None, "space", None, None, None), P()),
        out_specs=(block, block),
        check_vma=False,
    )
```

time: 215 us -> 78.4 us (0.36)
  waiting for transfers between devices: 95.2 us -> 0 us
  Pallas kernels: 0 us -> 70 us
  blocking collectives: 32.1 us -> 0 us
  matrix products: 24.9 us -> 0 us
  starting transfers between devices: 23.7 us -> 0 us
  between operations: 14.2 us -> 0.65 us
  other arithmetic: 11.6 us -> 0 us
  local copies, waits for them, and re-layouts: 13.4 us -> 7.55 us
    pallas_call x0 -> x1, Pallas kernels: none -> 70 us  [shards(): pl.pallas_call(body, name='gw', out_shape=(out, out), in_specs=[hbm, hbm,...]
    all_to_all x2 -> x0, waiting for transfers between devices: 47.7 us -> none  [the longest x1 25.1 us: shards(): lax.all_to_all(screen, 'energy', split_axis=2, concat_axis=2, tiled=True)]
    all_gather x1 -> x0, waiting for transfers between devices: 47.4 us -> none  [shards(): lax.all_gather(sigma_lesser, 'space', axis=2, tiled=True)]
    all_to_all x1 -> x0, blocking collectives: 32.1 us -> none  [shards(): lax.all_to_all(sigma_el, 'energy', split_axis=2, concat_axis=2, tiled=True)]
    dot_general x7 -> x0, matrix products: 24.9 us -> none  [the longest x1 14.1 us: shards(): jnp.einsum('ecnij,ednjl->encdil', own_row, lax.all_gather(sigma_lesser, '...]
    all_to_all x2 -> x0, starting transfers between devices: 23.4 us -> none  [the longest x1 15.1 us: shards(): lax.all_to_all(screen, 'energy', split_axis=2, concat_axis=2, tiled=True)]
    reshape x6 -> x0, local copies, waits for them, and re-layouts: 8.7 us -> none  [the longest x2 3.71 us: shards(): screen = w_lesser.reshape(energies_here, 2, groups, columns)]
    unnamed x10 -> x14, local copies, waits for them, and re-layouts: 1.71 us -> 7.55 us
  transfers between devices with their start and end apart: 3 -> 0, of which waited for: 3 -> 0; matrix products, arithmetic and copies ran while one was open for 4% -> 0% of each run, Pallas kernels for 0% -> 0%
where the time goes in v1:
time: 78.4 us; the launch traced here: 78.2 us
  Pallas kernels  70 us (89%)
  local copies, waits for them, and re-layouts  7.55 us (10%)
    pallas_call x1, Pallas kernels, shards(): pl.pallas_call(body, name='gw', out_shape=(out, out), in_specs=[hbm, hbm,...  70 us
    unnamed x14, local copies, waits for them, and re-layouts  7.55 us

profile of v1, /device:TPU:1, one launch (start us, length us, event | category | flops | bytes accessed | tf_op | source)
XLA Modules:
  0.0 78.2 jit_solution(14756855860803758466)
XLA Ops:
  0.6 0.0 copy-start
  0.6 1.2 %copy-done = bf16[1,2,1,512,512]{4,3,2,1,0:T(8,128)(2,1)S(1)} copy-done((bf16[1,2,1,512,512]{4,3,2,1,0:T(8,128)(2,1)S(1)}, bf16[1,2,1,512,512]{4,3,2,1,0:T(8,128)(2,1)}, u32[]{:S(2)}) %copy-start) | copy-done | bytes 1048600
  1.9 0.0 copy-start.1
  1.9 1.2 %copy-done.1 = bf16[1,2,1,512,512]{4,3,2,1,0:T(8,128)(2,1)S(1)} copy-done((bf16[1,2,1,512,512]{4,3,2,1,0:T(8,128)(2,1)S(1)}, bf16[1,2,1,512,512]{4,3,2,1,0:T(8,128)(2,1)}, u32[]{:S(2)}) %copy-start.1) | copy-done | bytes 1048600
  3.1 0.0 copy-start.2
  3.1 0.9 %copy-done.2 = bf16[2,128,192]{2,1,0:T(8,128)(2,1)S(1)} copy-done((bf16[2,128,192]{2,1,0:T(8,128)(2,1)S(1)}, bf16[2,128,192]{2,1,0:T(8,128)(2,1)}, u32[]{:S(2)}) %copy-start.2) | copy-done | bytes 98328
  4.0 0.0 copy-start.3
  4.0 0.9 %copy-done.3 = bf16[2,192,128]{2,1,0:T(8,128)(2,1)S(1)} copy-done((bf16[2,192,128]{2,1,0:T(8,128)(2,1)S(1)}, bf16[2,192,128]{2,1,0:T(8,128)(2,1)}, u32[]{:S(2)}) %copy-start.3) | copy-done | bytes 98328
  4.9 0.0 copy-start.4
  4.9 0.7 copy-done.4
  5.6 0.0 copy-start.5
  5.6 0.7 copy-done.5
  6.3 70.0 %gw.1 = (bf16[2,512,512]{2,1,0:T(8,128)(2,1)S(1)}, bf16[2,512,512]{2,1,0:T(8,128)(2,1)S(1)}) custom-call(bf16[2,512,512]{2,1,0:T(8,128)(2,1)S(1)} %bitcast.12, bf16[2,512,512]{2,1,0:T(8,128)(2,1)S(1)} %bitcast.13, bf16[8,512,512]{2,1,0:T(8,128)(2,1)} %bitcast.15, s32[1,64]{1,0:T(1,128)S(1)} %bitcast.14, bf16[2,192,128]{2,1,0:T(8,128)(2,1)S(1)} %copy-done.3, ...), custom_call_target="tpu_custom_call" | custom-call | tf_op jit(solution)/shard_map/gw/pallas_call | solution.py:286
  76.2 1.0 %copy.13 = bf16[1,2,1,512,512]{4,3,2,1,0:T(8,128)(2,1)} copy(bf16[1,2,1,512,512]{4,3,2,1,0:T(8,128)(2,1)S(1)} %bitcast.11) | data formatting | bytes 2097152
  77.2 1.0 %copy.14 = bf16[1,2,1,512,512]{4,3,2,1,0:T(8,128)(2,1)} copy(bf16[1,2,1,512,512]{4,3,2,1,0:T(8,128)(2,1)S(1)} %bitcast.10) | data formatting | bytes 2097152
Async XLA Ops:
  0.6 1.2 %copy-start = (bf16[1,2,1,512,512]{4,3,2,1,0:T(8,128)(2,1)S(1)}, bf16[1,2,1,512,512]{4,3,2,1,0:T(8,128)(2,1)}, u32[]{:S(2)}) copy-start(bf16[1,2,1,512,512]{4,3,2,1,0:T(8,128)(2,1)} %param.7) | copy-start | bytes 3145732
  1.9 1.2 %copy-start.1 = (bf16[1,2,1,512,512]{4,3,2,1,0:T(8,128)(2,1)S(1)}, bf16[1,2,1,512,512]{4,3,2,1,0:T(8,128)(2,1)}, u32[]{:S(2)}) copy-start(bf16[1,2,1,512,512]{4,3,2,1,0:T(8,128)(2,1)} %param.8) | copy-start | bytes 3145732
  3.1 0.9 %copy-start.2 = (bf16[2,128,192]{2,1,0:T(8,128)(2,1)S(1)}, bf16[2,128,192]{2,1,0:T(8,128)(2,1)}, u32[]{:S(2)}) copy-start(bf16[2,128,192]{2,1,0:T(8,128)(2,1)} %constant.7.clone.bt_ref) | copy-start | bytes 294916
  4.0 0.9 %copy-start.3 = (bf16[2,192,128]{2,1,0:T(8,128)(2,1)S(1)}, bf16[2,192,128]{2,1,0:T(8,128)(2,1)}, u32[]{:S(2)}) copy-start(bf16[2,192,128]{2,1,0:T(8,128)(2,1)} %constant.6.clone.ft_ref) | copy-start | bytes 294916
  4.9 0.7 copy-start.4
  5.6 0.7 copy-start.5

commit v2 on v1

v2 whole, which is shorter than its diff:
```python
import math

import jax
import jax.numpy as jnp
from jax import lax
from jax.experimental import pallas as pl
from jax.experimental.pallas import tpu as pltpu
from jax.sharding import PartitionSpec as P

MESH = pl.DeviceIdType.MESH
NE = 64
B = 512
T = 128
LEN = 96
TILES = (((0, 0), (0, 1)), ((2, 2), (0, 2)), ((1, 2), (2, 3)), ((0, 3), (1, 3)))
CHUNKS = len(TILES)
BF = jnp.bfloat16
F32 = jnp.float32


def mm(a, b):
    return jnp.dot(a, b, preferred_element_type=F32)


def body(g_hbm, w_hbm, r_hbm, idx_hbm, sig_ref, del_ref,
         g_v, w_v, idx_v, rc, rt, send, recv, ssend, u_v, scr, tmp,
         xb, ph, pw, fm, bm, ue, lcat, l3, x,
         lsem, gws, gwr, sgs, sgr, zs, zr, cs, cr):
    me = lax.axis_index("energy")
    sp = lax.axis_index("space")
    lo = sp // 2
    sp_core = lo * 2 + (sp + 1) % 2
    sp_z = (sp + 2) % 4
    sp_zc = (sp_core + 2) % 4
    order = (sp, sp_core, sp_z, sp_zc)
    zh = me // 4 % 4
    q_me = zh * 16 + me // 16 * 4 + me % 4
    za = zh
    zb = (zh + 3 + 2 * lo) % 4
    zc = (zh + 2) % 4
    zd = (zh + 1 + 2 * lo) % 4

    def ring(i):
        return lax.rem(me + i, NE)

    barrier = pltpu.get_barrier_semaphore()

    @pl.loop(1, NE)
    def _(i):
        pl.semaphore_signal(barrier, inc=1, device_id=(ring(i), sp), device_id_type=MESH)

    pl.semaphore_signal(barrier, inc=1, device_id=(me, sp_core), device_id_type=MESH)
    pl.semaphore_signal(barrier, inc=1, device_id=(me, sp_z), device_id_type=MESH)

    def tiles_of(h):
        for i, j in TILES[h]:
            for k in range(2 if i == j else 1):
                yield i + k, j + k

    def load(h, src, dst, i, j):
        at = (slice(None), slice(T * i, T * i + T), slice(T * j, T * j + T))
        return pltpu.make_async_copy(src.at[at], dst.at[at], lsem.at[h])

    for h in range(CHUNKS):
        for i, j in tiles_of(h):
            load(h, g_hbm, g_v, i, j).start()
            load(h, w_hbm, w_v, i, j).start()

    row = lax.broadcasted_iota(jnp.int32, (T, T), 0)
    col = lax.broadcasted_iota(jnp.int32, (T, T), 1)
    for h in range(CHUNKS):
        n_tiles = len(list(tiles_of(h)))
        all_of = g_v.at[:, 0:2 * T, 0:T * n_tiles]
        pltpu.make_async_copy(all_of, all_of, lsem.at[h]).wait()
        for t, (i, j) in enumerate(TILES[h]):
            for a, src in enumerate((g_v, w_v)):
                if i == j:
                    k = i + 1
                    d0r, d0i = (src[c, T * i:T * i + T, T * i:T * i + T].astype(F32) for c in range(2))
                    d1r, d1i = (src[c, T * k:T * k + T, T * k:T * k + T].astype(F32) for c in range(2))
                    both = (jnp.where(row < col, d0r, jnp.where(row > col, d1r, d1i)), jnp.where(row <= col, d0i, d1i))
                else:
                    both = [src[c, T * i:T * i + T, T * j:T * j + T].astype(F32) for c in range(2)]
                for c in range(2):
                    for n in range(4):
                        tmp[a, pl.ds(c * 4 + n, 32, stride=8), :] = both[c][32 * n:32 * n + 32]
                send[h, 32 * t:32 * t + 32, a] = tmp[a].reshape(32, 8, T).astype(BF)

        if h == 0:
            pl.semaphore_wait(barrier, NE + 1)

        @pl.loop(1, NE)
        def _(i):
            d = ring(i)
            q = lax.rem(lax.div(d, 4), 4) * 16 + lax.div(d, 16) * 4 + lax.rem(d, 4)
            pltpu.make_async_remote_copy(
                src_ref=send.at[h, q], dst_ref=recv.at[h, me], send_sem=gws.at[h], recv_sem=gwr.at[h],
                device_id=(d, sp), device_id_type=MESH).start()

        pltpu.make_async_copy(send.at[h, q_me], recv.at[h, me], gwr.at[h]).start()

    small = pltpu.make_async_copy(idx_hbm, idx_v, lsem.at[5])
    small.start()
    for n, k in enumerate(order):
        for c in range(2):
            for i in range(4):
                pltpu.make_async_copy(r_hbm.at[4 * c + k, :, T * i:T * i + T],
                                      rc.at[n, :, T * (2 * i + c):T * (2 * i + c) + T], lsem.at[4]).start()

    small.wait()

    def lines(shape, axis):
        return lax.broadcasted_iota(jnp.int32, shape, axis)

    twice = (lines((NE, T), 0) == lines((NE, T), 1) % NE).astype(F32).astype(BF)
    point = mm(jnp.broadcast_to(idx_v[...].astype(F32), (8, NE)).astype(BF), twice)[0:1, :]
    wide = (2 * LEN, T)
    out_c = (lines(wide, 0) >= LEN).astype(F32)
    freq = lines(wide, 0).astype(F32) - LEN * out_c
    in_c = (lines(wide, 1) >= NE).astype(F32)

    def wave(steps):
        turns = steps - LEN * jnp.floor((steps + 0.5) / LEN)
        return jnp.cos(turns * (2.0 * math.pi / LEN))

    def halves(m):
        high = m.astype(BF)
        return high, (m - high.astype(F32)).astype(BF)

    quarter = LEN // 4
    eye = (lines((2 * LEN, 2 * LEN), 0) == lines((2 * LEN, 2 * LEN), 1)).astype(F32).astype(BF)
    for a, m in enumerate(halves(wave(freq * point + quarter * (out_c - in_c)))):
        fm[a] = m
    for a, m in enumerate(halves(wave(freq * (point + NE // 2) + quarter * (1.0 - in_c + out_c)) * (NE**-0.5 / LEN))):
        bm[a] = lax.dot_general(m, eye, (((0,), (0,)), ((), ())), preferred_element_type=F32).astype(BF)

    pltpu.make_async_copy(rc, rc, lsem.at[4]).wait()

    @pl.loop(0, 4)
    def _(n):
        at = pl.multiple_of(n * 2 * T, 2 * T)
        for j in range(4):
            for i in range(4):
                r_t = rc[n, T * i:T * i + T, 2 * T * j:2 * T * j + T].astype(F32).T
                i_t = rc[n, T * i:T * i + T, 2 * T * j + T:2 * T * j + 2 * T].astype(F32).T
                rt[j, pl.ds(at, T), T * i:T * i + T] = r_t.astype(BF)
                rt[j, pl.ds(at, T), B + T * i:B + T * i + T] = (-i_t).astype(BF)
                rt[j, pl.ds(at + T, T), T * i:T * i + T] = i_t.astype(BF)
                rt[j, pl.ds(at + T, T), B + T * i:B + T * i + T] = r_t.astype(BF)

    def convolve(h):
        pltpu.make_async_copy(recv.at[h], recv.at[h], gwr.at[h]).wait()
        for a in range(2):
            scr[a] = recv[h, :, a].astype(F32).reshape(8 * NE, T)
        r = q_me % 32
        for a in range(2):
            diag = jnp.zeros((T, T), F32)
            for i in range(4):
                x_i = jnp.concatenate(
                    [scr[a, pl.ds(i, NE, stride=8), :], scr[a, pl.ds(4 + i, NE, stride=8), :]], axis=0)
                diag = jnp.where(col == 32 * i + r, x_i, diag)
                xb[a, :, T * i:T * i + T] = x_i.astype(BF)
            xb[a, :, 4 * T:5 * T] = jnp.where(row < NE, diag, 0.0).astype(BF)
            xb[a, :, 5 * T:] = jnp.where(row < NE, 0.0, diag).astype(BF)
        for n in range(3):
            cols = slice(256 * n, 256 * n + 256)
            gx = xb[0, :, cols]
            wx = xb[1, :, cols]
            gh = mm(fm[0], gx) + mm(fm[1], gx)
            wh = mm(fm[0], wx) + mm(fm[1], wx)
            pr = gh[:LEN] * wh[:LEN] - gh[LEN:] * wh[LEN:]
            pi = gh[:LEN] * wh[LEN:] + gh[LEN:] * wh[:LEN]
            prod = jnp.concatenate([pr, pi], axis=0)
            hi = prod.astype(BF)
            ph[:, cols] = hi
            pw[:, cols] = (prod - hi.astype(F32)).astype(BF)

        def back(cols):
            return mm(bm[0], ph[:, cols]) + mm(bm[1], ph[:, cols]) + mm(bm[0], pw[:, cols])

        y = back(slice(4 * T, 6 * T))
        fix = jnp.concatenate([-y[NE:, :T], y[NE:, T:]], axis=0)
        here = q_me < 32 if TILES[h][0][0] == TILES[h][0][1] else None
        for n in range(2):
            y = back(slice(256 * n, 256 * n + 256))
            for m in range(2):
                i = 2 * n + m
                z = y[:, T * m:T * m + T]
                if here is not None:
                    z = jnp.where((col == 32 * i + r) & here, fix, z)
                scr[0, pl.ds(i, NE, stride=8), :] = z[:NE]
                scr[0, pl.ds(4 + i, NE, stride=8), :] = z[NE:]
        ssend[h] = scr[0].reshape(NE, 8, T).astype(BF)

        @pl.loop(1, NE)
        def _(i):
            d = ring(i)
            far = lax.div(lax.rem(lax.rem(lax.div(d, 4), 4) - zh + 4 + lo, 4), 2)
            pltpu.make_async_remote_copy(
                src_ref=ssend.at[h, d], dst_ref=u_v.at[sp, h, q_me], send_sem=sgs.at[h], recv_sem=sgr.at[h],
                device_id=(d, lax.rem(sp + 2 * far, 4)), device_id_type=MESH).start()

        pltpu.make_async_copy(ssend.at[h, me], u_v.at[sp, h, q_me], sgr.at[h]).start()

    def part(k, h, z):
        return u_v.at[k, h, pl.ds(16 * z, 16)]

    def give(k, h, z, to, ss, rs):
        pltpu.make_async_remote_copy(
            src_ref=part(k, h, z), dst_ref=part(k, h, z), send_sem=ss, recv_sem=rs,
            device_id=(me, to), device_id_type=MESH).start()

    def whole(h, s):
        pltpu.make_async_copy(u_v.at[sp, h], u_v.at[sp, h], s).wait()

    first = ((sp, za), (sp, zb), (sp_z, zc), (sp_z, zb))
    second = ((sp, zc), (sp, zd), (sp_z, za), (sp_z, zd))

    def stage1(h):
        whole(h, sgr.at[h])
        for k, z in first:
            give(k, h, z, sp_z, zs.at[h], zr.at[h])
        for k, z in first:
            give(k, h, z, sp_core, cs.at[0, h], cr.at[0, h])

    def stage2(h):
        whole(h, zr.at[h])
        for k, z in second:
            give(k, h, z, sp_core, cs.at[1, h], cr.at[1, h])

    def stage3(h):
        whole(h, cr.at[0, h])
        whole(h, cr.at[1, h])

    def tile(k, h, t):
        tmp[t] = u_v[k, h, 32 * t:32 * t + 32].astype(F32).reshape(2 * T, T)
        return [jnp.concatenate([tmp[t, pl.ds(4 * c + n, 32, stride=8), :] for n in range(4)], axis=0) for c in range(2)]

    def put(n, at, p):
        ur, ui = p[0].astype(BF), p[1].astype(BF)
        ue[n, at:at + T, 0:T] = ur
        ue[n, at:at + T, T:2 * T] = ui
        ue[n, at + T:at + 2 * T, 0:T] = -ui
        ue[n, at + T:at + 2 * T, T:2 * T] = ur

    def upper(p):
        return (jnp.where(row < col, p[0], 0.0),
                jnp.where(row < col, p[1], jnp.where(row == col, 0.5 * p[1], 0.0)))

    def lower(p):
        return (jnp.where(row > col, p[0], 0.0),
                jnp.where(row > col, p[1], jnp.where(row == col, 0.5 * p[0], 0.0)))

    def left(n, i, depth):
        return mm(rc[n, :, 2 * T * i:2 * T * (i + depth)], ue[n, 2 * T * i:2 * T * (i + depth), :])

    def product(h):
        for n, k in enumerate(order):
            at = 2 * T * n
            p = tile(k, h, 0)
            s = tile(k, h, 1)
            if h == 0:
                put(n, 0, upper(p))
                lcat[:, at:at + 2 * T] = left(n, 0, 1).astype(BF)
                put(n, 0, s)
                put(n, 2 * T, lower(p))
                lcat[:, 1024 + at:1024 + at + 2 * T] = left(n, 0, 2).astype(BF)
            elif h == 2:
                d = tile(k, 1, 0)
                put(n, 0, tile(k, 1, 1))
                put(n, 2 * T, p)
                put(n, 4 * T, upper(d))
                lcat[:, at:at + 2 * T] = left(n, 0, 3).astype(BF)
                put(n, 4 * T, s)
                put(n, 6 * T, lower(d))
                l3[n] = left(n, 2, 2)
            else:
                put(n, 0, p)
                put(n, 2 * T, s)
                lcat[:, at:at + 2 * T] = (l3[n] + left(n, 0, 2)).astype(BF)

        for m in range(4):
            cols = slice(256 * m, 256 * m + 256)
            if h == 0:
                x[:, cols] = mm(lcat[:, :1024], rt[0, :, cols])
                x[:, cols] += mm(lcat[:, 1024:], rt[1, :, cols])
            else:
                x[:, cols] += mm(lcat[:, :1024], rt[2 if h == 2 else 3, :, cols])

    def sigma_out(h):
        for t, (i, j) in enumerate(TILES[h]):
            pr, pi = tile(sp, h, t)
            prt = pr.T
            pit = pi.T
            a = slice(T * i, T * i + T)
            if i == j:
                b = slice(T * i + T, T * i + 2 * T)
                sig_ref[0, a, a] = jnp.where(row < col, pr, jnp.where(row > col, -prt, 0.0)).astype(BF)
                sig_ref[1, a, a] = jnp.where(row <= col, pi, pit).astype(BF)
                sig_ref[0, b, b] = jnp.where(row > col, pr, jnp.where(row < col, -prt, 0.0)).astype(BF)
                sig_ref[1, b, b] = jnp.where(row > col, pi, jnp.where(row < col, pit, pr)).astype(BF)
            else:
                b = slice(T * j, T * j + T)
                sig_ref[0, a, b] = pr.astype(BF)
                sig_ref[1, a, b] = pi.astype(BF)
                sig_ref[0, b, a] = (-prt).astype(BF)
                sig_ref[1, b, a] = pit.astype(BF)

    for h in range(CHUNKS):
        convolve(h)
    stage1(0)
    stage1(1)
    stage2(0)
    stage1(2)
    stage2(1)
    stage3(0)
    product(0)
    stage1(3)
    stage2(2)
    stage3(1)
    stage3(2)
    sigma_out(0)
    sigma_out(1)
    product(2)
    stage2(3)
    sigma_out(2)
    sigma_out(3)
    stage3(3)
    product(3)

    for i in range(4):
        for j in range(i, 4):
            a = slice(T * i, T * i + T)
            b = slice(T * j, T * j + T)
            a2 = slice(B + T * i, B + T * i + T)
            b2 = slice(B + T * j, B + T * j + T)
            dr = x[a, b] - x[b, a].T
            di = x[a, b2] + x[b, a2].T
            del_ref[0, a, b] = dr.astype(BF)
            del_ref[1, a, b] = di.astype(BF)
            if i != j:
                del_ref[0, b, a] = (-dr.T).astype(BF)
                del_ref[1, b, a] = di.T.astype(BF)

    for h in range(CHUNKS):
        pltpu.make_async_copy(send.at[h, 0:NE - 1], send.at[h, 0:NE - 1], gws.at[h]).wait()
        pltpu.make_async_copy(ssend.at[h, 0:NE - 1], ssend.at[h, 0:NE - 1], sgs.at[h]).wait()
        whole(h, zs.at[h])
        whole(h, cs.at[0, h])
        whole(h, cs.at[1, h])


def shards(g, w, r, idx):
    vmem = pl.BlockSpec(memory_space=pltpu.VMEM)
    hbm = pl.BlockSpec(memory_space=pltpu.HBM)
    out = jax.ShapeDtypeStruct((2, B, B), BF)
    dma = pltpu.SemaphoreType.DMA
    sig, delta = pl.pallas_call(
        body,
        name="gw",
        out_shape=(out, out),
        in_specs=[hbm] * 4,
        out_specs=(vmem, vmem),
        scratch_shapes=[
            pltpu.VMEM((2, B, B), BF),
            pltpu.VMEM((2, B, B), BF),
            pltpu.VMEM((1, NE), jnp.int32),
            pltpu.VMEM((4, B, 2 * B), BF),
            pltpu.VMEM((4, 2 * B, 2 * B), BF),
            pltpu.VMEM((CHUNKS, NE, 2, 8, T), BF),
            pltpu.VMEM((CHUNKS, NE, 2, 8, T), BF),
            pltpu.VMEM((CHUNKS, NE, 8, T), BF),
            pltpu.VMEM((4, CHUNKS, NE, 8, T), BF),
            pltpu.VMEM((2, 8 * NE, T), F32),
            pltpu.VMEM((2, 2 * T, T), F32),
            pltpu.VMEM((2, T, 6 * T), BF),
            pltpu.VMEM((2 * LEN, 6 * T), BF),
            pltpu.VMEM((2 * LEN, 6 * T), BF),
            pltpu.VMEM((2, 2 * LEN, T), BF),
            pltpu.VMEM((2, T, 2 * LEN), BF),
            pltpu.VMEM((4, 8 * T, 2 * T), BF),
            pltpu.VMEM((B, 4 * B), BF),
            pltpu.VMEM((4, B, 2 * T), F32),
            pltpu.VMEM((B, 2 * B), F32),
            dma((6,)),
            dma((CHUNKS,)),
            dma((CHUNKS,)),
            dma((CHUNKS,)),
            dma((CHUNKS,)),
            dma((CHUNKS,)),
            dma((CHUNKS,)),
            dma((2, CHUNKS)),
            dma((2, CHUNKS)),
        ],
        compiler_params=pltpu.CompilerParams(collective_id=0, has_side_effects=True,
                                             vmem_limit_bytes=51 * 1024 * 1024),
    )(g.reshape(2, B, B), w.reshape(2, B, B), r.reshape(8, B, B), idx.reshape(1, NE))
    return sig.reshape(1, 2, 1, B, B), delta.reshape(1, 2, 1, B, B)


def solution(mesh):
    block = P("energy", None, "space", None, None)
    return jax.shard_map(
        shards,
        mesh=mesh,
        in_specs=(block, block, P("energy", None, "space", None, None, None), P()),
        out_specs=(block, block),
        check_vma=False,
    )
```

time: 78.4 us -> 67.5 us (0.86)
  Pallas kernels: 70 us -> 64.1 us
  local copies, waits for them, and re-layouts: 7.55 us -> 2.59 us
    pallas_call x1, Pallas kernels: 70 us -> 64.1 us  [shards(): pl.pallas_call(body, name='gw', out_shape=(out, out), in_specs=[hbm] * 4,...]
    unnamed x14 -> x4, local copies, waits for them, and re-layouts: 7.55 us -> 2.59 us
where the time goes in v2:
time: 67.5 us; the launch traced here: 67.4 us
  Pallas kernels  64.1 us (95%)
  local copies, waits for them, and re-layouts  2.59 us (4%)
    pallas_call x1, Pallas kernels, shards(): pl.pallas_call(body, name='gw', out_shape=(out, out), in_specs=[hbm] * 4,...  64.1 us
    unnamed x4, local copies, waits for them, and re-layouts  2.59 us

profile of v2, /device:TPU:1, one launch (start us, length us, event | category | flops | bytes accessed | tf_op | source)
XLA Modules:
  0.0 67.4 jit_solution(4609741171466936816)
XLA Ops:
  0.6 0.0 copy-start
  0.6 0.6 copy-done
  1.3 64.1 %gw.1 = (bf16[2,512,512]{2,1,0:T(8,128)(2,1)S(1)}, bf16[2,512,512]{2,1,0:T(8,128)(2,1)S(1)}) custom-call(bf16[2,512,512]{2,1,0:T(8,128)(2,1)} %bitcast.14, bf16[2,512,512]{2,1,0:T(8,128)(2,1)} %bitcast.15, bf16[8,512,512]{2,1,0:T(8,128)(2,1)} %bitcast.13, s32[1,64]{1,0:T(1,128)S(1)} %bitcast.12), custom_call_target="tpu_custom_call" | custom-call | tf_op jit(solution)/shard_map/gw/pallas_call | solution.py:358
  65.4 1.0 %copy.10 = bf16[1,2,1,512,512]{4,3,2,1,0:T(8,128)(2,1)} copy(bf16[1,2,1,512,512]{4,3,2,1,0:T(8,128)(2,1)S(1)} %bitcast.11) | data formatting | bytes 2097152
  66.4 1.0 %copy.11 = bf16[1,2,1,512,512]{4,3,2,1,0:T(8,128)(2,1)} copy(bf16[1,2,1,512,512]{4,3,2,1,0:T(8,128)(2,1)S(1)} %bitcast.10) | data formatting | bytes 2097152
Async XLA Ops:
  0.6 0.7 copy-start

commit v3 on v2

--- a/solution.py
+++ b/solution.py
@@ -32,7 +32,7 @@
     sp_core = lo * 2 + (sp + 1) % 2
     sp_z = (sp + 2) % 4
     sp_zc = (sp_core + 2) % 4
-    order = (sp, sp_core, sp_z, sp_zc)
+    order = (sp, sp_z, sp_core, sp_zc)
     zh = me // 4 % 4
     q_me = zh * 16 + me // 16 * 4 + me % 4
     za = zh
@@ -195,12 +195,14 @@
         @pl.loop(1, NE)
         def _(i):
             d = ring(i)
-            far = lax.div(lax.rem(lax.rem(lax.div(d, 4), 4) - zh + 4 + lo, 4), 2)
+            away = lax.rem((1 - 2 * lo) * (lax.rem(lax.div(d, 4), 4) - zh) + 4, 4)
+            far = lax.div(away, 2)
+            kind = away + far * (5 - 2 * away)
             pltpu.make_async_remote_copy(
-                src_ref=ssend.at[h, d], dst_ref=u_v.at[sp, h, q_me], send_sem=sgs.at[h], recv_sem=sgr.at[h],
+                src_ref=ssend.at[h, d], dst_ref=u_v.at[sp, h, q_me], send_sem=sgs.at[h], recv_sem=sgr.at[h, kind],
                 device_id=(d, lax.rem(sp + 2 * far, 4)), device_id_type=MESH).start()
 
-        pltpu.make_async_copy(ssend.at[h, me], u_v.at[sp, h, q_me], sgr.at[h]).start()
+        pltpu.make_async_copy(ssend.at[h, me], u_v.at[sp, h, q_me], sgr.at[h, 0]).start()
 
     def part(k, h, z):
         return u_v.at[k, h, pl.ds(16 * z, 16)]
@@ -213,19 +215,20 @@
     def whole(h, s):
         pltpu.make_async_copy(u_v.at[sp, h], u_v.at[sp, h], s).wait()
 
-    first = ((sp, za), (sp, zb), (sp_z, zc), (sp_z, zb))
-    second = ((sp, zc), (sp, zd), (sp_z, za), (sp_z, zd))
-
-    def stage1(h):
-        whole(h, sgr.at[h])
-        for k, z in first:
-            give(k, h, z, sp_z, zs.at[h], zr.at[h])
-        for k, z in first:
+    first = ((sp, za), (sp, zb), (sp_z, zb), (sp_z, zc))
+    second = ((sp_z, za), (sp_z, zd), (sp, zd), (sp, zc))
+
+    def stage1(h, kinds=range(4)):
+        for n in kinds:
+            k, z = first[n]
+            pltpu.make_async_copy(part(k, h, z), part(k, h, z), sgr.at[h, n]).wait()
+            give(k, h, z, sp_z, zs.at[h], zr.at[h, n])
             give(k, h, z, sp_core, cs.at[0, h], cr.at[0, h])
 
-    def stage2(h):
-        whole(h, zr.at[h])
-        for k, z in second:
+    def stage2(h, kinds=range(4)):
+        for n in kinds:
+            k, z = second[n]
+            pltpu.make_async_copy(part(k, h, z), part(k, h, z), zr.at[h, n]).wait()
             give(k, h, z, sp_core, cs.at[1, h], cr.at[1, h])
 
     def stage3(h):
@@ -254,38 +257,37 @@
     def left(n, i, depth):
         return mm(rc[n, :, 2 * T * i:2 * T * (i + depth)], ue[n, 2 * T * i:2 * T * (i + depth), :])
 
-    def product(h):
-        for n, k in enumerate(order):
-            at = 2 * T * n
-            p = tile(k, h, 0)
-            s = tile(k, h, 1)
-            if h == 0:
-                put(n, 0, upper(p))
-                lcat[:, at:at + 2 * T] = left(n, 0, 1).astype(BF)
-                put(n, 0, s)
-                put(n, 2 * T, lower(p))
-                lcat[:, 1024 + at:1024 + at + 2 * T] = left(n, 0, 2).astype(BF)
-            elif h == 2:
-                d = tile(k, 1, 0)
-                put(n, 0, tile(k, 1, 1))
-                put(n, 2 * T, p)
-                put(n, 4 * T, upper(d))
-                lcat[:, at:at + 2 * T] = left(n, 0, 3).astype(BF)
-                put(n, 4 * T, s)
-                put(n, 6 * T, lower(d))
-                l3[n] = left(n, 2, 2)
-            else:
-                put(n, 0, p)
-                put(n, 2 * T, s)
-                lcat[:, at:at + 2 * T] = (l3[n] + left(n, 0, 2)).astype(BF)
-
+    def place(n):
+        return slice(2 * T * n, 2 * T * n + 2 * T)
+
+    def rows01(n):
+        put(n, 0, upper(tile(order[n], 0, 0)))
+        lcat[:, place(n)] = left(n, 0, 1).astype(BF)
+        put(n, 0, tile(order[n], 0, 1))
+        put(n, 2 * T, lower(tile(order[n], 0, 0)))
+        lcat[:, place(4 + n)] = left(n, 0, 2).astype(BF)
+
+    def rows2(n):
+        put(n, 0, tile(order[n], 1, 1))
+        put(n, 2 * T, tile(order[n], 2, 0))
+        put(n, 4 * T, upper(tile(order[n], 1, 0)))
+        lcat[:, place(n)] = left(n, 0, 3).astype(BF)
+        put(n, 4 * T, tile(order[n], 2, 1))
+        put(n, 6 * T, lower(tile(order[n], 1, 0)))
+        l3[n] = left(n, 2, 2)
+
+    def rows3(n):
+        put(n, 0, tile(order[n], 3, 0))
+        put(n, 2 * T, tile(order[n], 3, 1))
+        lcat[:, place(4 + n)] = (l3[n] + left(n, 0, 2)).astype(BF)
+
+    def total(j, at, depth):
+        k = slice(2 * T * at, 2 * T * (at + depth))
+        c = slice(1024 * (j % 2) + 2 * T * at, 1024 * (j % 2) + 2 * T * (at + depth))
         for m in range(4):
             cols = slice(256 * m, 256 * m + 256)
-            if h == 0:
-                x[:, cols] = mm(lcat[:, :1024], rt[0, :, cols])
-                x[:, cols] += mm(lcat[:, 1024:], rt[1, :, cols])
-            else:
-                x[:, cols] += mm(lcat[:, :1024], rt[2 if h == 2 else 3, :, cols])
+            y = mm(lcat[:, c], rt[j, k, cols])
+            x[:, cols] = y if j == 0 else x[:, cols] + y
 
     def sigma_out(h):
         for t, (i, j) in enumerate(TILES[h]):
@@ -306,27 +308,47 @@
                 sig_ref[0, b, a] = (-prt).astype(BF)
                 sig_ref[1, b, a] = pit.astype(BF)
 
-    for h in range(CHUNKS):
-        convolve(h)
-    stage1(0)
-    stage1(1)
+    convolve(0)
+    convolve(1)
+    stage1(0, (0,))
+    convolve(2)
+    stage1(1, (0,))
+    convolve(3)
+    stage1(2, (0,))
+    stage1(0, (1, 2, 3))
+    stage1(1, (1, 2, 3))
     stage2(0)
-    stage1(2)
+    rows01(0)
+    rows01(1)
+    stage1(3, (0,))
+    stage1(2, (1, 2, 3))
     stage2(1)
+    sigma_out(0)
+    sigma_out(1)
     stage3(0)
-    product(0)
-    stage1(3)
+    rows01(2)
+    rows01(3)
+    total(0, 0, 4)
+    stage1(3, (1, 2, 3))
     stage2(2)
+    total(1, 0, 4)
+    rows2(0)
+    rows2(1)
+    stage2(3)
     stage3(1)
     stage3(2)
-    sigma_out(0)
-    sigma_out(1)
-    product(2)
-    stage2(3)
+    rows2(2)
+    rows2(3)
+    total(2, 0, 4)
+    rows3(0)
+    rows3(1)
+    total(3, 0, 2)
     sigma_out(2)
     sigma_out(3)
     stage3(3)
-    product(3)
+    rows3(2)
+    rows3(3)
+    total(3, 2, 2)
 
     for i in range(4):
         for j in range(i, 4):
@@ -386,9 +408,9 @@
             dma((CHUNKS,)),
             dma((CHUNKS,)),
             dma((CHUNKS,)),
+            dma((CHUNKS, 4)),
             dma((CHUNKS,)),
-            dma((CHUNKS,)),
-            dma((CHUNKS,)),
+            dma((CHUNKS, 4)),
             dma((2, CHUNKS)),
             dma((2, CHUNKS)),
         ],

time: 67.5 us -> 63.6 us (0.942)
  Pallas kernels: 64.1 us -> 60 us
    pallas_call x1, Pallas kernels: 64.1 us -> 60 us  [shards(): pl.pallas_call(body, name='gw', out_shape=(out, out), in_specs=[hbm] * 4,...]
where the time goes in v3:
time: 63.6 us; the launch traced here: 63.2 us
  Pallas kernels  60 us (94%)
  local copies, waits for them, and re-layouts  2.59 us (4%)
  between operations  0.65 us (1%)
    pallas_call x1, Pallas kernels, shards(): pl.pallas_call(body, name='gw', out_shape=(out, out), in_specs=[hbm] * 4,...  60 us
    unnamed x4, local copies, waits for them, and re-layouts  2.59 us

profile of v3, /device:TPU:1, one launch (start us, length us, event | category | flops | bytes accessed | tf_op | source)
XLA Modules:
  0.0 63.2 jit_solution(13315941569710752262)
XLA Ops:
  0.6 0.0 copy-start
  0.6 0.6 %copy-done = s32[64]{0:T(128)S(1)} copy-done((s32[64]{0:T(128)S(1)}, s32[64]{0:T(128)}, u32[]{:S(2)}) %copy-start) | copy-done | bytes 280
  1.3 60.0 %gw.1 = (bf16[2,512,512]{2,1,0:T(8,128)(2,1)S(1)}, bf16[2,512,512]{2,1,0:T(8,128)(2,1)S(1)}) custom-call(bf16[2,512,512]{2,1,0:T(8,128)(2,1)} %bitcast.14, bf16[2,512,512]{2,1,0:T(8,128)(2,1)} %bitcast.15, bf16[8,512,512]{2,1,0:T(8,128)(2,1)} %bitcast.13, s32[1,64]{1,0:T(1,128)S(1)} %bitcast.12), custom_call_target="tpu_custom_call" | custom-call | tf_op jit(solution)/shard_map/gw/pallas_call | solution.py:380
  61.3 1.0 %copy.10 = bf16[1,2,1,512,512]{4,3,2,1,0:T(8,128)(2,1)} copy(bf16[1,2,1,512,512]{4,3,2,1,0:T(8,128)(2,1)S(1)} %bitcast.11) | data formatting | bytes 2097152
  62.2 1.0 %copy.11 = bf16[1,2,1,512,512]{4,3,2,1,0:T(8,128)(2,1)} copy(bf16[1,2,1,512,512]{4,3,2,1,0:T(8,128)(2,1)S(1)} %bitcast.10) | data formatting | bytes 2097152
Async XLA Ops:
  0.6 0.7 %copy-start = (s32[64]{0:T(128)S(1)}, s32[64]{0:T(128)}, u32[]{:S(2)}) copy-start(s32[64]{0:T(128)} %param.7) | copy-start | bytes 772

commit v4 on v3

--- a/solution.py
+++ b/solution.py
@@ -22,9 +22,9 @@
     return jnp.dot(a, b, preferred_element_type=F32)
 
 
-def body(g_hbm, w_hbm, r_hbm, idx_hbm, sig_ref, del_ref,
+def body(g_hbm, w_hbm, r_hbm, idx_hbm, sig_ref, xr, xi,
          g_v, w_v, idx_v, rc, rt, send, recv, ssend, u_v, scr, tmp,
-         xb, ph, pw, fm, bm, ue, lcat, l3, x,
+         xb, ph, pw, fm, bm, ue, lcat, l3,
          lsem, gws, gwr, sgs, sgr, zs, zr, cs, cr):
     me = lax.axis_index("energy")
     sp = lax.axis_index("space")
@@ -287,7 +287,9 @@
         for m in range(4):
             cols = slice(256 * m, 256 * m + 256)
             y = mm(lcat[:, c], rt[j, k, cols])
-            x[:, cols] = y if j == 0 else x[:, cols] + y
+            half = slice(256 * (m % 2), 256 * (m % 2) + 256)
+            x = (xr, xi)[m // 2]
+            x[:, half] = y if j == 0 else x[:, half] + y
 
     def sigma_out(h):
         for t, (i, j) in enumerate(TILES[h]):
@@ -350,20 +352,6 @@
     rows3(3)
     total(3, 2, 2)
 
-    for i in range(4):
-        for j in range(i, 4):
-            a = slice(T * i, T * i + T)
-            b = slice(T * j, T * j + T)
-            a2 = slice(B + T * i, B + T * i + T)
-            b2 = slice(B + T * j, B + T * j + T)
-            dr = x[a, b] - x[b, a].T
-            di = x[a, b2] + x[b, a2].T
-            del_ref[0, a, b] = dr.astype(BF)
-            del_ref[1, a, b] = di.astype(BF)
-            if i != j:
-                del_ref[0, b, a] = (-dr.T).astype(BF)
-                del_ref[1, b, a] = di.T.astype(BF)
-
     for h in range(CHUNKS):
         pltpu.make_async_copy(send.at[h, 0:NE - 1], send.at[h, 0:NE - 1], gws.at[h]).wait()
         pltpu.make_async_copy(ssend.at[h, 0:NE - 1], ssend.at[h, 0:NE - 1], sgs.at[h]).wait()
@@ -372,17 +360,37 @@
         whole(h, cs.at[1, h])
 
 
+def results(sig_v, xr, xi, sig_ref, del_ref, out, sem):
+    moves = [pltpu.make_async_copy(sig_v, sig_ref, sem.at[4])]
+    moves[0].start()
+    for i in range(4):
+        a = slice(T * i, T * i + T)
+        for j in range(i, 4):
+            b = slice(T * j, T * j + T)
+            dr = xr[a, b] - xr[b, a].T
+            di = xi[a, b] + xi[b, a].T
+            out[0, a, b] = dr.astype(BF)
+            out[1, a, b] = di.astype(BF)
+            if i != j:
+                out[0, b, a] = (-dr.T).astype(BF)
+                out[1, b, a] = di.T.astype(BF)
+        moves.append(pltpu.make_async_copy(out.at[:, a, :], del_ref.at[:, a, :], sem.at[i]))
+        moves[-1].start()
+    for move in moves:
+        move.wait()
+
+
 def shards(g, w, r, idx):
     vmem = pl.BlockSpec(memory_space=pltpu.VMEM)
     hbm = pl.BlockSpec(memory_space=pltpu.HBM)
     out = jax.ShapeDtypeStruct((2, B, B), BF)
     dma = pltpu.SemaphoreType.DMA
-    sig, delta = pl.pallas_call(
+    sig, xr, xi = pl.pallas_call(
         body,
         name="gw",
-        out_shape=(out, out),
+        out_shape=(out,) + (jax.ShapeDtypeStruct((B, B), F32),) * 2,
         in_specs=[hbm] * 4,
-        out_specs=(vmem, vmem),
+        out_specs=(vmem,) * 3,
         scratch_shapes=[
             pltpu.VMEM((2, B, B), BF),
             pltpu.VMEM((2, B, B), BF),
@@ -403,7 +411,6 @@
             pltpu.VMEM((4, 8 * T, 2 * T), BF),
             pltpu.VMEM((B, 4 * B), BF),
             pltpu.VMEM((4, B, 2 * T), F32),
-            pltpu.VMEM((B, 2 * B), F32),
             dma((6,)),
             dma((CHUNKS,)),
             dma((CHUNKS,)),
@@ -415,8 +422,17 @@
             dma((2, CHUNKS)),
         ],
         compiler_params=pltpu.CompilerParams(collective_id=0, has_side_effects=True,
-                                             vmem_limit_bytes=51 * 1024 * 1024),
+                                             vmem_limit_bytes=50 * 1024 * 1024),
     )(g.reshape(2, B, B), w.reshape(2, B, B), r.reshape(8, B, B), idx.reshape(1, NE))
+    sig, delta = pl.pallas_call(
+        results,
+        name="results",
+        out_shape=(out, out),
+        in_specs=[vmem] * 3,
+        out_specs=(pl.BlockSpec(memory_space=pl.ANY),) * 2,
+        scratch_shapes=[pltpu.VMEM((2, B, B), BF), dma((5,))],
+        compiler_params=pltpu.CompilerParams(vmem_limit_bytes=16 * 1024 * 1024),
+    )(sig, xr, xi)
     return sig.reshape(1, 2, 1, B, B), delta.reshape(1, 2, 1, B, B)
 
 

time: 63.6 us -> 63.1 us (level)
  local copies, waits for them, and re-layouts: 2.59 us -> 0.65 us
  Pallas kernels: 60 us -> 61.2 us
    unnamed x4 -> x2, local copies, waits for them, and re-layouts: 2.59 us -> 0.65 us
    pallas_call x1 -> x2, Pallas kernels: 60 us -> 61.2 us  [the longest x1 59.6 us: shards(): pl.pallas_call(body, name='gw', out_shape=(out,) + (jax.ShapeDtypeStruct(...]
where the time goes in v4:
time: 63.1 us; the launch traced here: 62.7 us
  Pallas kernels  61.2 us (97%)
  between operations  0.81 us (1%)
  local copies, waits for them, and re-layouts  0.65 us (1%)
    pallas_call x1, Pallas kernels, shards(): pl.pallas_call(body, name='gw', out_shape=(out,) + (jax.ShapeDtypeStruct(...  59.6 us
    pallas_call x1, Pallas kernels, shards(): pl.pallas_call(results, name='results', out_shape=(out, out), in_specs=[v...  1.62 us

profile of v4, /device:TPU:1, one launch (start us, length us, event | category | flops | bytes accessed | tf_op | source)
XLA Modules:
  0.0 62.7 jit_solution(8083048029489893801)
XLA Ops:
  0.6 0.0 copy-start
  0.6 0.6 %copy-done = s32[64]{0:T(128)S(1)} copy-done((s32[64]{0:T(128)S(1)}, s32[64]{0:T(128)}, u32[]{:S(2)}) %copy-start) | copy-done | bytes 280
  1.3 59.6 %gw.1 = (bf16[2,512,512]{2,1,0:T(8,128)(2,1)S(1)}, f32[512,512]{1,0:T(8,128)S(1)}, f32[512,512]{1,0:T(8,128)S(1)}) custom-call(bf16[2,512,512]{2,1,0:T(8,128)(2,1)} %bitcast.12, bf16[2,512,512]{2,1,0:T(8,128)(2,1)} %bitcast.13, bf16[8,512,512]{2,1,0:T(8,128)(2,1)} %bitcast.11, s32[1,64]{1,0:T(1,128)S(1)} %bitcast.10), custom_call_target="tpu_custom_call" | custom-call | tf_op jit(solution)/shard_map/gw/pallas_call | solution.py:388
  60.9 1.6 %results.1 = (bf16[2,512,512]{2,1,0:T(8,128)(2,1)}, bf16[2,512,512]{2,1,0:T(8,128)(2,1)}) custom-call(bf16[2,512,512]{2,1,0:T(8,128)(2,1)S(1)} %get-tuple-element.7.sig_v, f32[512,512]{1,0:T(8,128)S(1)} %get-tuple-element.8.xr, f32[512,512]{1,0:T(8,128)S(1)} %get-tuple-element.9.xi), custom_call_target="tpu_custom_call" | custom-call | tf_op jit(solution)/shard_map/results/pallas_call | solution.py:427
Async XLA Ops:
  0.6 0.7 %copy-start = (s32[64]{0:T(128)S(1)}, s32[64]{0:T(128)}, u32[]{:S(2)}) copy-start(s32[64]{0:T(128)} %param.7) | copy-start | bytes 772

commit v5 on v4

--- a/solution.py
+++ b/solution.py
@@ -24,7 +24,7 @@
 
 def body(g_hbm, w_hbm, r_hbm, idx_hbm, sig_ref, xr, xi,
          g_v, w_v, idx_v, rc, rt, send, recv, ssend, u_v, scr, tmp,
-         xb, ph, pw, fm, bm, ue, lcat, l3,
+         xb, ph, pw, fm, bm, ue, lcat, l2, l3,
          lsem, gws, gwr, sgs, sgr, zs, zr, cs, cr):
     me = lax.axis_index("energy")
     sp = lax.axis_index("space")
@@ -267,14 +267,19 @@
         put(n, 2 * T, lower(tile(order[n], 0, 0)))
         lcat[:, place(4 + n)] = left(n, 0, 2).astype(BF)
 
+    def rows2_early(n):
+        d = tile(order[n], 1, 0)
+        put(n, 0, tile(order[n], 1, 1))
+        put(n, 4 * T, upper(d))
+        put(n, 6 * T, lower(d))
+        l2[n] = left(n, 0, 1) + left(n, 2, 1)
+        l3[n] = left(n, 3, 1)
+
     def rows2(n):
-        put(n, 0, tile(order[n], 1, 1))
         put(n, 2 * T, tile(order[n], 2, 0))
-        put(n, 4 * T, upper(tile(order[n], 1, 0)))
-        lcat[:, place(n)] = left(n, 0, 3).astype(BF)
         put(n, 4 * T, tile(order[n], 2, 1))
-        put(n, 6 * T, lower(tile(order[n], 1, 0)))
-        l3[n] = left(n, 2, 2)
+        lcat[:, place(n)] = (l2[n] + left(n, 1, 1)).astype(BF)
+        l3[n] += left(n, 2, 1)
 
     def rows3(n):
         put(n, 0, tile(order[n], 3, 0))
@@ -330,14 +335,18 @@
     stage3(0)
     rows01(2)
     rows01(3)
+    rows2_early(0)
+    rows2_early(1)
     total(0, 0, 4)
     stage1(3, (1, 2, 3))
     stage2(2)
     total(1, 0, 4)
+    stage3(1)
+    rows2_early(2)
+    rows2_early(3)
     rows2(0)
     rows2(1)
     stage2(3)
-    stage3(1)
     stage3(2)
     rows2(2)
     rows2(3)
@@ -411,6 +420,7 @@
             pltpu.VMEM((4, 8 * T, 2 * T), BF),
             pltpu.VMEM((B, 4 * B), BF),
             pltpu.VMEM((4, B, 2 * T), F32),
+            pltpu.VMEM((4, B, 2 * T), F32),
             dma((6,)),
             dma((CHUNKS,)),
             dma((CHUNKS,)),

time: 63.1 us -> 63.1 us (level)
  no operation moved by 1% of the time
where the time goes in v5:
time: 63.1 us; the launch traced here: 62.7 us
  Pallas kernels  61.3 us (97%)
  between operations  0.81 us (1%)
  local copies, waits for them, and re-layouts  0.65 us (1%)
    pallas_call x1, Pallas kernels, shards(): pl.pallas_call(body, name='gw', out_shape=(out,) + (jax.ShapeDtypeStruct(...  59.6 us
    pallas_call x1, Pallas kernels, shards(): pl.pallas_call(results, name='results', out_shape=(out, out), in_specs=[v...  1.62 us

profile of v5, /device:TPU:1, one launch (start us, length us, event | category | flops | bytes accessed | tf_op | source)
XLA Modules:
  0.0 62.7 jit_solution(12136788224848511656)
XLA Ops:
  0.6 0.0 copy-start
  0.6 0.6 %copy-done = s32[64]{0:T(128)S(1)} copy-done((s32[64]{0:T(128)S(1)}, s32[64]{0:T(128)}, u32[]{:S(2)}) %copy-start) | copy-done | bytes 280
  1.3 59.6 %gw.1 = (bf16[2,512,512]{2,1,0:T(8,128)(2,1)S(1)}, f32[512,512]{1,0:T(8,128)S(1)}, f32[512,512]{1,0:T(8,128)S(1)}) custom-call(bf16[2,512,512]{2,1,0:T(8,128)(2,1)} %bitcast.12, bf16[2,512,512]{2,1,0:T(8,128)(2,1)} %bitcast.13, bf16[8,512,512]{2,1,0:T(8,128)(2,1)} %bitcast.11, s32[1,64]{1,0:T(1,128)S(1)} %bitcast.10), custom_call_target="tpu_custom_call" | custom-call | tf_op jit(solution)/shard_map/gw/pallas_call | solution.py:397
  60.9 1.6 %results.1 = (bf16[2,512,512]{2,1,0:T(8,128)(2,1)}, bf16[2,512,512]{2,1,0:T(8,128)(2,1)}) custom-call(bf16[2,512,512]{2,1,0:T(8,128)(2,1)S(1)} %get-tuple-element.7.sig_v, f32[512,512]{1,0:T(8,128)S(1)} %get-tuple-element.8.xr, f32[512,512]{1,0:T(8,128)S(1)} %get-tuple-element.9.xi), custom_call_target="tpu_custom_call" | custom-call | tf_op jit(solution)/shard_map/results/pallas_call | solution.py:437
Async XLA Ops:
  0.6 0.7 %copy-start = (s32[64]{0:T(128)S(1)}, s32[64]{0:T(128)}, u32[]{:S(2)}) copy-start(s32[64]{0:T(128)} %param.7) | copy-start | bytes 772
